TPU v7x, 128 devices: a whole 4x4x4 slice. The times are simulated.
128 devices in a mesh: seq: 8 (over x_lo, z), exp: 16 (over x_hi, y, core).
Axes of the slice: x: 4 (x_hi: 2, x_lo: 2; x = x_hi * 2 + x_lo), y: 4, z: 4, core: 2. Of those that a mesh axis runs over, the one named last changes fastest.
Arguments:
- tokens: bfloat16 [16, 1024, 2048], P('exp', 'seq'), may hold values from -6 to 6
- position_of_row: int32 [16, 1024], P('exp'), may hold values from 0 to 1023, each once within a row
- request_of_position: int32 [16, 1024], P('exp'), may hold values from 0 to 3, never falling along the last dimension, each value on 1 to 512 neighbouring positions
- expert_ids: int32 [16, 1024, 6], P('exp', 'seq'), may hold values from 0 to 63, all different within a row; in each aligned block of 128 rows (0 to 127, 128 to 255, ..., all dimensions but the last counted through in order) at most 16 rows name the same one
- gate_values: float32 [16, 1024, 6], P('exp', 'seq'), may hold values from 0.1 to 1
- attn_norm: bfloat16 [2048], replicated, may hold values from 0.25 to 1.75
- moe_norm: bfloat16 [2048], replicated, may hold values from 0.25 to 1.75
- w_query: bfloat16 [2048, 2048], P(None, 'seq'), may hold values from -0.125 to 0.125
- w_latent: bfloat16 [2048, 512], replicated, may hold values from -0.125 to 0.125
- w_key_up: bfloat16 [512, 2048], P(None, 'seq'), may hold values from -120 to 120
- w_value_up: bfloat16 [512, 2048], P(None, 'seq'), may hold values from -0.25 to 0.25
- w_output: bfloat16 [2048, 2048], P('seq'), may hold values from -0.125 to 0.125
- w_shared_gate: bfloat16 [2048, 2816], P(None, 'seq'), may hold values from -0.125 to 0.125
- w_shared_up: bfloat16 [2048, 2816], P(None, 'seq'), may hold values from -0.125 to 0.125
- w_shared_down: bfloat16 [2816, 2048], P('seq'), may hold values from -0.109375 to 0.109375
- w_routed_gate: bfloat16 [128, 2048, 704], P(('seq', 'exp')), may hold values from -0.125 to 0.125
- w_routed_up: bfloat16 [128, 2048, 704], P(('seq', 'exp')), may hold values from -0.125 to 0.125
- w_routed_down: bfloat16 [128, 704, 2048], P(('seq', 'exp')), may hold values from -0.15625 to 0.15625
Outputs:
- layer_out: bfloat16 [16, 1024, 2048], P('exp', 'seq')
Inputs may be any that keep to these rules, and one draw needn't show every extreme that they name: `expert_ids`: each row names 6 different experts; among the rows of one device no expert is named by more than 16 rows, and some expert reaches 16 on some device. `position_of_row`: each row of a group holds a different position. `request_of_position`: never falls along positions; each request holds 1 to 512 positions.
All inputs are finite; a program needn't handle non-finite values.
Results may differ from a plain program's by a relative error of at most 0.027.
The roundings to bfloat16 on the way count: a program that leaves them out, or rounds other values in their place, can miss the bound.
Values may be sent and summed in bfloat16 or wider, within the bound.
No kernel may reach another device: no remote copies, remote signals or barrier semaphores. Data moves between devices by JAX's collectives and lax.ppermute only.
A program may use at most 128 MiB of HBM per device.

v0:
```python
import jax
import jax.numpy as jnp
from jax import lax
from jax.sharding import PartitionSpec as P

HD = 128
LAT = 512
epsilon = 1e-06
score_scale = 192.0 ** (-0.5)


def rms_scale(values, gain):
    widened = values.astype(jnp.float32)
    mean_square = jnp.mean(widened * widened, axis=-1, keepdims=True)
    return (widened * lax.rsqrt(mean_square + epsilon) * gain.astype(jnp.float32)).astype(
        jnp.bfloat16
    )


def swiglu_rows(rows_in, gate_weight, up_weight):
    gate_proj = jnp.dot(rows_in, gate_weight, preferred_element_type=jnp.float32)
    up_proj = jnp.dot(rows_in, up_weight, preferred_element_type=jnp.float32)
    return (jax.nn.silu(gate_proj) * up_proj).astype(jnp.bfloat16)


def shards(
    tokens,
    position_of_row,
    request_of_position,
    expert_ids,
    gate_values,
    attn_norm,
    moe_norm,
    w_query,
    w_latent,
    w_key_up,
    w_value_up,
    w_output,
    w_shared_gate,
    w_shared_up,
    w_shared_down,
    w_routed_gate,
    w_routed_up,
    w_routed_down,
):
    rows_here = tokens[0]
    row_count = rows_here.shape[0]
    width = rows_here.shape[1]
    heads_here = w_query.shape[1] // HD
    normed = rms_scale(rows_here, attn_norm)
    piece_rows = lax.all_gather(normed, "seq", axis=0, tiled=True)
    queries = jnp.dot(piece_rows, w_query, preferred_element_type=jnp.float32).astype(jnp.bfloat16)
    queries = queries.reshape(piece_rows.shape[0], heads_here, HD)
    key_heads = w_key_up.reshape(LAT, heads_here, HD)
    queries_query_latent = jnp.einsum(
        "rhk,lhk->rhl", queries, key_heads, preferred_element_type=jnp.float32
    ).astype(jnp.bfloat16)
    query_all = queries_query_latent.reshape(piece_rows.shape[0], heads_here * LAT)
    latent_own = jnp.dot(normed, w_latent, preferred_element_type=jnp.float32).astype(jnp.bfloat16)
    latent_all = lax.all_gather(latent_own, "seq", axis=0, tiled=True)
    positions = position_of_row[0]
    requests = jnp.take(request_of_position[0], positions)
    allowed = (requests[:, None] == requests[None, :]) & (positions[None, :] <= positions[:, None])
    head_outputs = []
    for head in range(heads_here):
        query_latent = query_all[:, head * LAT : (head + 1) * LAT]
        scores = (
            jnp.dot(query_latent, latent_all.T, preferred_element_type=jnp.float32) * score_scale
        )
        scores = jnp.where(allowed, scores, -1e30)
        largest = jnp.max(scores, axis=1, keepdims=True)
        raised = jnp.exp(scores - largest)
        probs = (raised / jnp.sum(raised, axis=1, keepdims=True)).astype(jnp.bfloat16)
        mixed = jnp.dot(probs, latent_all, preferred_element_type=jnp.float32).astype(jnp.bfloat16)
        value_head = w_value_up[:, head * HD : (head + 1) * HD]
        head_outputs.append(
            jnp.dot(mixed, value_head, preferred_element_type=jnp.float32).astype(jnp.bfloat16)
        )
    joined = jnp.concatenate(head_outputs, axis=1)
    row_block = joined
    attended = lax.psum_scatter(
        jnp.dot(row_block, w_output, preferred_element_type=jnp.float32),
        "seq",
        scatter_dimension=0,
        tiled=True,
    )
    resid = (rows_here.astype(jnp.float32) + attended).astype(jnp.bfloat16)
    moe_in = rms_scale(resid, moe_norm)
    shared_hidden = swiglu_rows(
        lax.all_gather(moe_in, "seq", axis=0, tiled=True), w_shared_gate, w_shared_up
    )
    row_block = shared_hidden
    shared_out = lax.psum_scatter(
        jnp.dot(row_block, w_shared_down, preferred_element_type=jnp.float32).astype(jnp.bfloat16),
        "seq",
        scatter_dimension=0,
        tiled=True,
    ).astype(jnp.float32)
    seq_count = lax.axis_size("seq")
    exp_count = lax.axis_size("exp")
    devices = seq_count * exp_count
    experts = devices // 2
    highest = expert_ids.shape[2]
    capacity = row_count * highest * 4 // (3 * experts)
    expert_list = expert_ids[0].reshape(row_count * highest)
    onehot = (expert_list[:, None] == jnp.arange(experts, dtype=jnp.int32)[None, :]).astype(
        jnp.int32
    )
    earlier = jnp.cumsum(onehot, axis=0) - onehot
    slot_index = jnp.sum(earlier * onehot, axis=1)
    place = expert_list * capacity + slot_index
    outgoing = (
        jnp.zeros((experts * capacity, width), jnp.bfloat16)
        .at[place]
        .set(jnp.repeat(moe_in, highest, axis=0))
    )
    doubled = jnp.repeat(outgoing.reshape(experts, capacity, width), 2, axis=0)
    arrived = lax.all_to_all(doubled, ("seq", "exp"), split_axis=0, concat_axis=0, tiled=True)
    flattened = arrived.reshape(-1, width)
    activated = swiglu_rows(flattened, w_routed_gate[0], w_routed_up[0])
    half_out = jnp.dot(activated, w_routed_down[0], preferred_element_type=jnp.float32).astype(
        jnp.bfloat16
    )
    partial_value = half_out.reshape(arrived.shape)
    returned = lax.all_to_all(
        partial_value, ("seq", "exp"), split_axis=0, concat_axis=0, tiled=True
    )
    halves = returned.reshape(experts, 2, capacity, width).astype(jnp.float32)
    expert_out = (halves[:, 0] + halves[:, 1]).astype(jnp.bfloat16)
    picked = jnp.take(expert_out.reshape(experts * capacity, width), place, axis=0)
    picked = picked.astype(jnp.float32).reshape(row_count, highest, width)
    routed_out = jnp.sum(picked * gate_values[0][:, :, None], axis=1)
    layer_out = (resid.astype(jnp.float32) + shared_out + routed_out).astype(jnp.bfloat16)
    return layer_out.reshape(1, row_count, width)


def solution(mesh):
    in_specs = (
        P("exp", "seq", None),
        P("exp", None),
        P("exp", None),
        P("exp", "seq", None),
        P("exp", "seq", None),
        P(),
        P(),
        P(None, "seq"),
        P(),
        P(None, "seq"),
        P(None, "seq"),
        P("seq", None),
        P(None, "seq"),
        P(None, "seq"),
        P("seq", None),
        P(("seq", "exp"), None, None),
        P(("seq", "exp"), None, None),
        P(("seq", "exp"), None, None),
    )
    out_specs = P("exp", "seq", None)
    return jax.shard_map(shards, mesh=mesh, in_specs=in_specs, out_specs=out_specs, check_vma=False)
```

profile of v0, /device:TPU:8, one launch (start us, length us, event | category | flops | bytes accessed | tf_op | source)
XLA Modules:
  0.0 670.7 jit_solution(1113696121236296590)
XLA Ops:
  13.8 4.5 gather_fusion
  18.4 47.6 %all-gather.4.cloned.1.call-done = bf16[1024,2048]{1,0:T(8,128)(2,1)} async-done(((bf16[128,2048]{1,0:T(8,128)(2,1)}), bf16[1024,2048]{1,0:T(8,128)(2,1)}) %all-gather.4.cloned.1.call-update) | async-done | bytes 4194320 | tf_op jit(solution)/shard_map/all_gather | solution.py:51
  71.8 33.6 %all-gather.6.cloned.1.call-done = bf16[1024,512]{1,0:T(8,128)(2,1)} async-done(((bf16[128,512]{1,0:T(8,128)(2,1)}), bf16[1024,512]{1,0:T(8,128)(2,1)}) %all-gather.6.cloned.1.call-update) | async-done | bytes 1048592 | tf_op jit(solution)/shard_map/all_gather | solution.py:60
  116.1 4.1 fusion.20
  120.2 4.1 fusion.19
  124.3 5.7 fusion.34
  131.9 4.9 reduce-window.6
  139.4 82.8 %reduce-scatter.3.cloned.1.call-done = f32[128,2048]{1,0:T(8,128)} async-done(((f32[1024,2048]{1,0:T(8,128)}), f32[128,2048]{1,0:T(8,128)}) %reduce-scatter.3.cloned.1.call-update) | async-done | bytes 1048592 | tf_op jit(solution)/shard_map/reduce_scatter | solution.py:81
  227.3 6.3 reshape.203
  233.6 10.4 %scatter_custom_fusion = bf16[1024,2048]{1,0:T(8,128)(2,1)} fusion(s32[768]{0:T(1024)S(1)} %fusion.46, bf16[768,2048]{1,0:T(8,128)(2,1)} %reshape.203, bf16[]{:T(256)} %constant.57.clone.1), kind=kCustom, calls=%fused_computation.25 | custom fusion | bytes 4194816 | tf_op jit(solution)/shard_map/scatter | solution.py:115
  244.1 6.8 %broadcast_in_dim.50 = bf16[64,2,16,2048]{3,2,1,0:T(8,128)(2,1)} broadcast(bf16[64,16,2048]{2,1,0:T(8,128)(2,1)} %bitcast.100), dimensions={0,2,3} | broadcast | bytes 12582912 | tf_op jit(solution)/shard_map/broadcast_in_dim | solution.py:117
  250.8 7.3 %all-to-all-start = ((bf16[128,16,2048]{2,1,0:T(8,128)(2,1)}), bf16[128,16,2048]{2,1,0:T(8,128)(2,1)}, u32[]{:S(2)}, u32[]{:S(2)}) async-start(bf16[128,16,2048]{2,1,0:T(8,128)(2,1)} %bitcast.99), calls=%async_computation.2 | async-start | bytes 16777216 | tf_op jit(solution)/shard_map/all_to_all | solution.py:118
  258.7 130.7 %all-to-all-done = bf16[128,16,2048]{2,1,0:T(8,128)(2,1)} async-done(((bf16[128,16,2048]{2,1,0:T(8,128)(2,1)}), bf16[128,16,2048]{2,1,0:T(8,128)(2,1)}, u32[]{:S(2)}, u32[]{:S(2)}) %all-to-all-start) | async-done | bytes 8388640 | tf_op jit(solution)/shard_map/all_to_all | solution.py:118
  389.4 11.2 %fusion.7 = f32[2048,704]{0,1:T(8,128)} fusion(bf16[2048,2048]{1,0:T(8,128)(2,1)} %bitcast.16, bf16[1,2048,704]{1,2,0:T(8,128)(2,1)} %param.33), kind=kOutput, calls=%fused_computation.22 | convolution fusion | flops 5905580032 | bytes 17039360 | tf_op jit(solution)/shard_map/dot_general | solution.py:21
  400.6 19.1 %convolution_convert_fusion = bf16[2048,2048]{1,0:T(8,128)(2,1)} fusion(f32[2048,704]{0,1:T(8,128)} %fusion.7, bf16[2048,2048]{1,0:T(8,128)(2,1)} %bitcast.16, bf16[1,704,2048]{2,1,0:T(8,128)(2,1)S(1)} %copy-done, bf16[1,2048,704]{1,2,0:T(8,128)(2,1)} %param.34), kind=kOutput, calls=%fused_computation.8 | convolution fusion | flops 11824005120 | bytes 28311552 | tf_op jit(solution)/shard_map/dot_general | solution.py:121
  419.7 43.2 %all-to-all-start.1 = ((bf16[128,16,2048]{2,1,0:T(8,128)(2,1)}), bf16[128,16,2048]{2,1,0:T(8,128)(2,1)}, u32[]{:S(2)}, u32[]{:S(2)}) async-start(bf16[128,16,2048]{2,1,0:T(8,128)(2,1)} %bitcast.101), calls=%async_computation.3 | async-start | bytes 16777216 | tf_op jit(solution)/shard_map/all_to_all | solution.py:125
  463.2 5.2 fusion.53
  468.4 9.0 %convolution_convert_fusion.1 = bf16[1024,2048]{1,0:T(8,128)(2,1)} fusion(bf16[352,2048]{1,0:T(8,128)(2,1)S(1)} %copy-done.16, bf16[1024,2048]{1,0:T(8,128)(2,1)} %all-gather.8.cloned.1.call-done, bf16[2048,352]{0,1:T(8,128)(2,1)} %param.31, f32[1024,352]{0,1:T(8,128)} %fusion.53), kind=kOutput, calls=%fused_computation.17 | convolution fusion | flops 2957049856 | bytes 12713984 | tf_op jit(solution)/shard_map/dot_general | solution.py:94
  478.2 140.0 %all-to-all-done.1 = bf16[128,16,2048]{2,1,0:T(8,128)(2,1)} async-done(((bf16[128,16,2048]{2,1,0:T(8,128)(2,1)}), bf16[128,16,2048]{2,1,0:T(8,128)(2,1)}, u32[]{:S(2)}, u32[]{:S(2)}) %all-to-all-start.1) | async-done | bytes 8388640 | tf_op jit(solution)/shard_map/all_to_all | solution.py:125
  618.2 11.3 %convert.3 = f32[64,2,16,2048]{3,2,1,0:T(8,128)} convert(bf16[64,2,16,2048]{3,2,1,0:T(8,128)(2,1)} %bitcast.22) | non-fusion elementwise | flops 4194304 | bytes 25165824 | tf_op jit(solution)/shard_map/convert_element_type | solution.py:128
  629.5 8.8 %fusion.1 = bf16[64,1,16,2048]{3,2,0,1:T(8,128)(2,1)} fusion(f32[64,2,16,2048]{3,2,1,0:T(8,128)} %convert.3), kind=kLoop, calls=%fused_computation.5 | loop fusion | flops 4194304 | bytes 20971520 | tf_op jit(solution)/shard_map/convert_element_type | solution.py:129
  638.3 9.8 %gather_fusion.1 = bf16[768,2048]{1,0:T(8,128)(2,1)} fusion(bf16[1024,2048]{1,0:T(8,128)(2,1)} %bitcast.98, s32[1024]{0:T(1024)S(1)} %pad_clamp_fusion), kind=kCustom, calls=%fused_computation.1 | custom fusion | bytes 6294528 | tf_op jit(solution)/shard_map/jit(_take)/gather | solution.py:130
  648.1 6.4 gather.15
  654.6 7.0 %multiply_reduce_fusion = f32[128,2048]{1,0:T(8,128)} fusion(f32[128,6]{1,0:T(8,128)S(1)} %bitcast.105, bf16[128,6,2048]{2,1,0:T(8,128)(2,1)} %gather.15, pred[128,6]{1,0:T(8,128)(4,1)S(1)} %copy.41), kind=kLoop, calls=%fused_computation.7 | loop fusion | flops 6029312 | bytes 4198144 | tf_op jit(solution)/shard_map/reduce_sum | solution.py:132
  (86 shorter events, 37.1 us)
Async XLA Ops:
  6.5 394.0 %copy-start = (bf16[1,704,2048]{2,1,0:T(8,128)(2,1)S(1)}, bf16[1,704,2048]{2,1,0:T(8,128)(2,1)}, u32[]{:S(2)}) copy-start(bf16[1,704,2048]{2,1,0:T(8,128)(2,1)} %param.35) | copy-start | bytes 8650756
  6.5 7.2 %copy-start.11 = (s32[1,1024]{1,0:T(1,128)S(1)}, s32[1,1024]{1,0:T(1,128)}, u32[]{:S(2)}) copy-start(s32[1,1024]{1,0:T(1,128)} %param.19) | copy-start | bytes 12292
  6.5 7.2 %copy-start.2 = (s32[1,1024]{1,0:T(1,128)S(1)}, s32[1,1024]{1,0:T(1,128)}, u32[]{:S(2)}) copy-start(s32[1,1024]{1,0:T(1,128)} %param.20) | copy-start | bytes 12292
  6.5 59.4 %all-gather.4.cloned.1.call-start = ((), (), s32[]{:S(2)}) async-start(), calls=%async_computation.4 | async-start | bytes 4718592 | tf_op jit(solution)/shard_map/all_gather | solution.py:51
  10.7 94.7 %all-gather.6.cloned.1.call-start = ((), (), s32[]{:S(2)}) async-start(), calls=%async_computation.5 | async-start | bytes 1179648 | tf_op jit(solution)/shard_map/all_gather | solution.py:60
  13.7 208.5 %reduce-scatter.3.cloned.1.call-start = ((), (), s32[]{:S(2)}) async-start(), calls=%async_computation.6 | async-start | bytes 9437184 | tf_op jit(solution)/shard_map/reduce_scatter | solution.py:81
  18.3 51.4 %copy-start.10 = (bf16[512,256]{1,0:T(8,128)(2,1)S(1)}, bf16[512,256]{1,0:T(8,128)(2,1)}, u32[]{:S(2)}) copy-start(bf16[512,256]{1,0:T(8,128)(2,1)} %param.27) | copy-start | bytes 786436
  108.6 5.0 copy-start.7
  108.6 3.1 copy-start.9
  108.6 3.4 copy-start.17
  113.6 1.9 copy-start.8
  130.1 0.7 copy-start.12
  130.1 1.1 copy-start.13
  130.1 92.1 %copy-start.3 = (bf16[1,128,2048]{2,1,0:T(8,128)(2,1)S(1)}, bf16[1,128,2048]{2,1,0:T(8,128)(2,1)}, u32[]{:S(2)}) copy-start(bf16[1,128,2048]{2,1,0:T(8,128)(2,1)} %param.18) | copy-start | bytes 1572868
  223.7 0.8 copy-start.4
  224.7 8.9 %copy-start.6 = (bf16[128,2048]{1,0:T(8,128)(2,1)}, bf16[128,2048]{1,0:T(8,128)(2,1)S(1)}, u32[]{:S(2)}) copy-start(bf16[128,2048]{1,0:T(8,128)(2,1)S(1)} %fusion.23) | copy-start | bytes 1572868
  250.8 138.5 %all-to-all-start = ((bf16[128,16,2048]{2,1,0:T(8,128)(2,1)}), bf16[128,16,2048]{2,1,0:T(8,128)(2,1)}, u32[]{:S(2)}, u32[]{:S(2)}) async-start(bf16[128,16,2048]{2,1,0:T(8,128)(2,1)} %bitcast.99), calls=%async_computation.2 | async-start | bytes 16777216 | tf_op jit(solution)/shard_map/all_to_all | solution.py:118
  258.1 205.1 %all-gather.8.cloned.1.call-start = ((), (), s32[]{:S(2)}) async-start(), calls=%async_computation.7 | async-start | bytes 4718592 | tf_op jit(solution)/shard_map/all_gather | solution.py:90
  419.7 43.5 %copy-start.15 = (bf16[2048,352]{0,1:T(8,128)(2,1)S(1)}, bf16[2048,352]{0,1:T(8,128)(2,1)}, u32[]{:S(2)}) copy-start(bf16[2048,352]{0,1:T(8,128)(2,1)} %param.30) | copy-start | bytes 4325380
  419.7 198.6 %all-to-all-start.1 = ((bf16[128,16,2048]{2,1,0:T(8,128)(2,1)}), bf16[128,16,2048]{2,1,0:T(8,128)(2,1)}, u32[]{:S(2)}, u32[]{:S(2)}) async-start(bf16[128,16,2048]{2,1,0:T(8,128)(2,1)} %bitcast.101), calls=%async_computation.3 | async-start | bytes 16777216 | tf_op jit(solution)/shard_map/all_to_all | solution.py:125
  462.9 5.5 copy-start.16
  462.9 198.6 %reduce-scatter.5.cloned.1.call-start = ((), (), s32[]{:S(2)}) async-start(), calls=%async_computation.8 | async-start | bytes 4718592 | tf_op jit(solution)/shard_map/reduce_scatter | solution.py:93
  648.1 15.7 %copy-start.1 = (bf16[1,704,2048]{2,1,0:T(8,128)(2,1)S(1)}, bf16[1,704,2048]{2,1,0:T(8,128)(2,1)}, u32[]{:S(2)}) copy-start(bf16[1,704,2048]{2,1,0:T(8,128)(2,1)} %param.35) | copy-start | bytes 8650756
  654.6 7.0 %copy-start.5 = (bf16[128,2048]{1,0:T(8,128)(2,1)S(1)}, bf16[128,2048]{1,0:T(8,128)(2,1)}, u32[]{:S(2)}) copy-start(bf16[128,2048]{1,0:T(8,128)(2,1)} %copy-done.4) | copy-start | bytes 1572868
  (1 other events, 0.7 us)
Sparse Core Ops, SparseCore 0:
  10.9 55.0 all-gather.3
  67.6 37.7 all-gather.5
  130.2 91.9 reduce-scatter.2
  260.3 144.3 all-gather.7
  477.5 143.9 reduce-scatter.4
where the time goes:
time: 680 us; the launch traced here: 671 us
  waiting for transfers between devices  435 us (64%)
  matrix products  71.9 us (11%)
  local copies, waits for them, and re-layouts  55.6 us (8%)
  starting transfers between devices  50.9 us (7%)
  other arithmetic  43.3 us (6%)
  between operations  13.7 us (2%)
    all_to_all x1, waiting for transfers between devices, shards(): lax.all_to_all(partial_value, ('seq', 'exp'), split_axis=0, concat_axis=0...  140 us
    all_to_all x1, waiting for transfers between devices, shards(): lax.all_to_all(doubled, ('seq', 'exp'), split_axis=0, concat_axis=0, tile...  131 us
    reduce_scatter x1, waiting for transfers between devices, shards(): lax.psum_scatter(jnp.dot(row_block, w_output, preferred_element_type=jnp....  82.8 us
    all_gather x1, waiting for transfers between devices, shards(): piece_rows = lax.all_gather(normed, 'seq', axis=0, tiled=True)  47.6 us
    all_to_all x1, starting transfers between devices, shards(): lax.all_to_all(partial_value, ('seq', 'exp'), split_axis=0, concat_axis=0...  43.2 us
    all_gather x1, waiting for transfers between devices, shards(): latent_all = lax.all_gather(latent_own, 'seq', axis=0, tiled=True)  33.6 us
    dot_general x1, matrix products, shards(): jnp.dot(activated, w_routed_down[0], preferred_element_type=jnp.float32)  19.1 us
    dot_general x2, matrix products, swiglu_rows(): jnp.dot(rows_in, gate_weight, preferred_element_type=jnp.float32)  16.4 us
  transfers between devices with their start and end apart: 7, of which 5 were waited for; matrix products, arithmetic and copies ran while one was open for 16% of the time, Pallas kernels for 0%

commit v1 on v0

--- a/solution.py
+++ b/solution.py
@@ -57,7 +57,13 @@
     ).astype(jnp.bfloat16)
     query_all = queries_query_latent.reshape(piece_rows.shape[0], heads_here * LAT)
     latent_own = jnp.dot(normed, w_latent, preferred_element_type=jnp.float32).astype(jnp.bfloat16)
-    latent_all = lax.all_gather(latent_own, "seq", axis=0, tiled=True)
+    check_core = lambda x0, bus_axis: jnp.concatenate(
+        lax.all_to_all(
+            jnp.stack([x0 for _ in range(lax.axis_size(bus_axis))], axis=0), bus_axis, 0, 0
+        ),
+        0,
+    )
+    latent_all = check_core(latent_own, "seq")
     positions = position_of_row[0]
     requests = jnp.take(request_of_position[0], positions)
     allowed = (requests[:, None] == requests[None, :]) & (positions[None, :] <= positions[:, None])

time: 680 us -> 659 us (0.969)
  waiting for transfers between devices: 435 us -> 409 us
    all_gather x1 -> x0, waiting for transfers between devices: 33.6 us -> none  [shards(): latent_all = lax.all_gather(latent_own, 'seq', axis=0, tiled=True)]
  transfers between devices with their start and end apart: 7 -> 7, of which waited for: 5 -> 4; matrix products, arithmetic and copies ran while one was open for 16% -> 17% of each run, Pallas kernels for 0% -> 0%
where the time goes in v1:
time: 659 us; the launch traced here: 649 us
  waiting for transfers between devices  409 us (62%)
  matrix products  75.3 us (11%)
  starting transfers between devices  54 us (8%)
  local copies, waits for them, and re-layouts  52 us (8%)
  other arithmetic  45.5 us (7%)
  between operations  13.7 us (2%)
    all_to_all x1, waiting for transfers between devices, shards(): lax.all_to_all(partial_value, ('seq', 'exp'), split_axis=0, concat_axis=0...  140 us
    all_to_all x1, waiting for transfers between devices, shards(): lax.all_to_all(doubled, ('seq', 'exp'), split_axis=0, concat_axis=0, tile...  134 us
    reduce_scatter x1, waiting for transfers between devices, shards(): lax.psum_scatter(jnp.dot(row_block, w_output, preferred_element_type=jnp....  82.9 us
    all_gather x1, waiting for transfers between devices, shards(): piece_rows = lax.all_gather(normed, 'seq', axis=0, tiled=True)  51 us
    all_to_all x1, starting transfers between devices, shards(): lax.all_to_all(partial_value, ('seq', 'exp'), split_axis=0, concat_axis=0...  40.1 us
    dot_general x1, matrix products, shards(): jnp.dot(activated, w_routed_down[0], preferred_element_type=jnp.float32)  19.1 us
    dot_general x2, matrix products, swiglu_rows(): jnp.dot(rows_in, gate_weight, preferred_element_type=jnp.float32)  16.4 us
    gather x2, local copies, waits for them, and re-layouts, shards(): jnp.take(expert_out.reshape(experts * capacity, width), place, axis=0)  16.3 us
  transfers between devices with their start and end apart: 7, of which 4 were waited for; matrix products, arithmetic and copies ran while one was open for 17% of the time, Pallas kernels for 0%

profile of v1, /device:TPU:8, one launch (start us, length us, event | category | flops | bytes accessed | tf_op | source)
XLA Modules:
  0.0 649.1 jit_solution(2189730739884686604)
XLA Ops:
  14.0 6.2 all-to-all-start
  20.4 4.5 gather_fusion
  24.9 51.0 %all-gather.3.cloned.1.call-done = bf16[1024,2048]{1,0:T(8,128)(2,1)} async-done(((bf16[128,2048]{1,0:T(8,128)(2,1)}), bf16[1024,2048]{1,0:T(8,128)(2,1)}) %all-gather.3.cloned.1.call-update) | async-done | bytes 4194320 | tf_op jit(solution)/shard_map/all_gather | solution.py:51
  85.2 5.5 fusion.51
  91.3 4.1 fusion.20
  102.3 5.7 fusion.34
  109.9 4.9 reduce-window.6
  117.4 82.9 %reduce-scatter.3.cloned.1.call-done = f32[128,2048]{1,0:T(8,128)} async-done(((f32[1024,2048]{1,0:T(8,128)}), f32[128,2048]{1,0:T(8,128)}) %reduce-scatter.3.cloned.1.call-update) | async-done | bytes 1048592 | tf_op jit(solution)/shard_map/reduce_scatter | solution.py:87
  205.4 6.3 reshape.209
  211.7 10.4 %scatter_custom_fusion = bf16[1024,2048]{1,0:T(8,128)(2,1)} fusion(s32[768]{0:T(1024)S(1)} %fusion.46, bf16[768,2048]{1,0:T(8,128)(2,1)} %reshape.209, bf16[]{:T(256)} %constant.57.clone.1), kind=kCustom, calls=%fused_computation.25 | custom fusion | bytes 4194816 | tf_op jit(solution)/shard_map/scatter | solution.py:121
  222.1 6.8 %broadcast_in_dim.50 = bf16[64,2,16,2048]{3,2,1,0:T(8,128)(2,1)} broadcast(bf16[64,16,2048]{2,1,0:T(8,128)(2,1)} %bitcast.101), dimensions={0,2,3} | broadcast | bytes 12582912 | tf_op jit(solution)/shard_map/broadcast_in_dim | solution.py:123
  228.9 7.3 %all-to-all-start.1 = ((bf16[128,16,2048]{2,1,0:T(8,128)(2,1)}), bf16[128,16,2048]{2,1,0:T(8,128)(2,1)}, u32[]{:S(2)}, u32[]{:S(2)}) async-start(bf16[128,16,2048]{2,1,0:T(8,128)(2,1)} %bitcast.100), calls=%async_computation.3 | async-start | bytes 16777216 | tf_op jit(solution)/shard_map/all_to_all | solution.py:124
  236.9 134.2 %all-to-all-done.1 = bf16[128,16,2048]{2,1,0:T(8,128)(2,1)} async-done(((bf16[128,16,2048]{2,1,0:T(8,128)(2,1)}), bf16[128,16,2048]{2,1,0:T(8,128)(2,1)}, u32[]{:S(2)}, u32[]{:S(2)}) %all-to-all-start.1) | async-done | bytes 8388640 | tf_op jit(solution)/shard_map/all_to_all | solution.py:124
  371.1 11.2 %fusion.7 = f32[2048,704]{0,1:T(8,128)} fusion(bf16[2048,2048]{1,0:T(8,128)(2,1)} %bitcast.17, bf16[1,2048,704]{1,2,0:T(8,128)(2,1)} %param.33), kind=kOutput, calls=%fused_computation.22 | convolution fusion | flops 5905580032 | bytes 17039360 | tf_op jit(solution)/shard_map/dot_general | solution.py:21
  382.3 19.1 %convolution_convert_fusion = bf16[2048,2048]{1,0:T(8,128)(2,1)} fusion(f32[2048,704]{0,1:T(8,128)} %fusion.7, bf16[2048,2048]{1,0:T(8,128)(2,1)} %bitcast.17, bf16[1,704,2048]{2,1,0:T(8,128)(2,1)S(1)} %copy-done, bf16[1,2048,704]{1,2,0:T(8,128)(2,1)} %param.34), kind=kOutput, calls=%fused_computation.8 | convolution fusion | flops 11824005120 | bytes 28311552 | tf_op jit(solution)/shard_map/dot_general | solution.py:127
  401.4 40.1 %all-to-all-start.2 = ((bf16[128,16,2048]{2,1,0:T(8,128)(2,1)}), bf16[128,16,2048]{2,1,0:T(8,128)(2,1)}, u32[]{:S(2)}, u32[]{:S(2)}) async-start(bf16[128,16,2048]{2,1,0:T(8,128)(2,1)} %bitcast.102), calls=%async_computation.4 | async-start | bytes 16777216 | tf_op jit(solution)/shard_map/all_to_all | solution.py:131
  441.8 5.2 fusion.53
  447.0 9.0 %convolution_convert_fusion.1 = bf16[1024,2048]{1,0:T(8,128)(2,1)} fusion(bf16[352,2048]{1,0:T(8,128)(2,1)S(1)} %copy-done.15, bf16[1024,2048]{1,0:T(8,128)(2,1)} %all-gather.5.cloned.1.call-done, bf16[2048,352]{0,1:T(8,128)(2,1)} %param.31, f32[1024,352]{0,1:T(8,128)} %fusion.53), kind=kOutput, calls=%fused_computation.17 | convolution fusion | flops 2957049856 | bytes 12713984 | tf_op jit(solution)/shard_map/dot_general | solution.py:100
  456.8 139.8 %all-to-all-done.2 = bf16[128,16,2048]{2,1,0:T(8,128)(2,1)} async-done(((bf16[128,16,2048]{2,1,0:T(8,128)(2,1)}), bf16[128,16,2048]{2,1,0:T(8,128)(2,1)}, u32[]{:S(2)}, u32[]{:S(2)}) %all-to-all-start.2) | async-done | bytes 8388640 | tf_op jit(solution)/shard_map/all_to_all | solution.py:131
  596.7 11.3 %convert.3 = f32[64,2,16,2048]{3,2,1,0:T(8,128)} convert(bf16[64,2,16,2048]{3,2,1,0:T(8,128)(2,1)} %bitcast.23) | non-fusion elementwise | flops 4194304 | bytes 25165824 | tf_op jit(solution)/shard_map/convert_element_type | solution.py:134
  608.0 8.8 %fusion.1 = bf16[64,1,16,2048]{3,2,0,1:T(8,128)(2,1)} fusion(f32[64,2,16,2048]{3,2,1,0:T(8,128)} %convert.3), kind=kLoop, calls=%fused_computation.5 | loop fusion | flops 4194304 | bytes 20971520 | tf_op jit(solution)/shard_map/convert_element_type | solution.py:135
  616.8 9.8 %gather_fusion.1 = bf16[768,2048]{1,0:T(8,128)(2,1)} fusion(bf16[1024,2048]{1,0:T(8,128)(2,1)} %bitcast.99, s32[1024]{0:T(1024)S(1)} %pad_clamp_fusion), kind=kCustom, calls=%fused_computation.1 | custom fusion | bytes 6294528 | tf_op jit(solution)/shard_map/jit(_take)/gather | solution.py:136
  626.6 6.4 gather.15
  633.0 7.0 %multiply_reduce_fusion = f32[128,2048]{1,0:T(8,128)} fusion(f32[128,6]{1,0:T(8,128)S(1)} %bitcast.106, bf16[128,6,2048]{2,1,0:T(8,128)(2,1)} %gather.15, pred[128,6]{1,0:T(8,128)(4,1)S(1)} %copy.41), kind=kLoop, calls=%fused_computation.7 | loop fusion | flops 6029312 | bytes 4198144 | tf_op jit(solution)/shard_map/reduce_sum | solution.py:138
  (82 shorter events, 37.8 us)
Async XLA Ops:
  6.5 375.8 %copy-start = (bf16[1,704,2048]{2,1,0:T(8,128)(2,1)S(1)}, bf16[1,704,2048]{2,1,0:T(8,128)(2,1)}, u32[]{:S(2)}) copy-start(bf16[1,704,2048]{2,1,0:T(8,128)(2,1)} %param.35) | copy-start | bytes 8650756
  6.5 13.8 %copy-start.10 = (s32[1,1024]{1,0:T(1,128)S(1)}, s32[1,1024]{1,0:T(1,128)}, u32[]{:S(2)}) copy-start(s32[1,1024]{1,0:T(1,128)} %param.19) | copy-start | bytes 12292
  6.5 13.8 %copy-start.2 = (s32[1,1024]{1,0:T(1,128)S(1)}, s32[1,1024]{1,0:T(1,128)}, u32[]{:S(2)}) copy-start(s32[1,1024]{1,0:T(1,128)} %param.20) | copy-start | bytes 12292
  6.5 69.5 %all-gather.3.cloned.1.call-start = ((), (), s32[]{:S(2)}) async-start(), calls=%async_computation.5 | async-start | bytes 4718592 | tf_op jit(solution)/shard_map/all_gather | solution.py:51
  14.0 67.8 %all-to-all-start = ((bf16[8,128,512]{2,1,0:T(8,128)(2,1)}), bf16[8,128,512]{2,1,0:T(8,128)(2,1)}, u32[]{:S(2)}, u32[]{:S(2)}) async-start(bf16[8,128,512]{2,1,0:T(8,128)(2,1)} %stack.2), calls=%async_computation | async-start | bytes 2097152 | tf_op jit(solution)/shard_map/all_to_all | solution.py:61
  20.3 180.0 %reduce-scatter.3.cloned.1.call-start = ((), (), s32[]{:S(2)}) async-start(), calls=%async_computation.6 | async-start | bytes 9437184 | tf_op jit(solution)/shard_map/reduce_scatter | solution.py:87
  24.9 54.8 %copy-start.9 = (bf16[512,256]{1,0:T(8,128)(2,1)S(1)}, bf16[512,256]{1,0:T(8,128)(2,1)}, u32[]{:S(2)}) copy-start(bf16[512,256]{1,0:T(8,128)(2,1)} %param.27) | copy-start | bytes 786436
  81.8 3.3 copy-start.8
  85.2 5.5 copy-start.7
  108.1 0.7 copy-start.11
  108.1 1.1 copy-start.12
  108.1 92.2 %copy-start.3 = (bf16[1,128,2048]{2,1,0:T(8,128)(2,1)S(1)}, bf16[1,128,2048]{2,1,0:T(8,128)(2,1)}, u32[]{:S(2)}) copy-start(bf16[1,128,2048]{2,1,0:T(8,128)(2,1)} %param.18) | copy-start | bytes 1572868
  201.8 0.8 copy-start.4
  202.8 8.9 %copy-start.6 = (bf16[128,2048]{1,0:T(8,128)(2,1)}, bf16[128,2048]{1,0:T(8,128)(2,1)S(1)}, u32[]{:S(2)}) copy-start(bf16[128,2048]{1,0:T(8,128)(2,1)S(1)} %fusion.23) | copy-start | bytes 1572868
  228.9 142.2 %all-to-all-start.1 = ((bf16[128,16,2048]{2,1,0:T(8,128)(2,1)}), bf16[128,16,2048]{2,1,0:T(8,128)(2,1)}, u32[]{:S(2)}, u32[]{:S(2)}) async-start(bf16[128,16,2048]{2,1,0:T(8,128)(2,1)} %bitcast.100), calls=%async_computation.3 | async-start | bytes 16777216 | tf_op jit(solution)/shard_map/all_to_all | solution.py:124
  236.2 205.6 %all-gather.5.cloned.1.call-start = ((), (), s32[]{:S(2)}) async-start(), calls=%async_computation.7 | async-start | bytes 4718592 | tf_op jit(solution)/shard_map/all_gather | solution.py:96
  401.4 40.4 %copy-start.14 = (bf16[2048,352]{0,1:T(8,128)(2,1)S(1)}, bf16[2048,352]{0,1:T(8,128)(2,1)}, u32[]{:S(2)}) copy-start(bf16[2048,352]{0,1:T(8,128)(2,1)} %param.30) | copy-start | bytes 4325380
  401.4 195.3 %all-to-all-start.2 = ((bf16[128,16,2048]{2,1,0:T(8,128)(2,1)}), bf16[128,16,2048]{2,1,0:T(8,128)(2,1)}, u32[]{:S(2)}, u32[]{:S(2)}) async-start(bf16[128,16,2048]{2,1,0:T(8,128)(2,1)} %bitcast.102), calls=%async_computation.4 | async-start | bytes 16777216 | tf_op jit(solution)/shard_map/all_to_all | solution.py:131
  441.5 5.5 copy-start.15
  441.5 198.4 %reduce-scatter.5.cloned.1.call-start = ((), (), s32[]{:S(2)}) async-start(), calls=%async_computation.8 | async-start | bytes 4718592 | tf_op jit(solution)/shard_map/reduce_scatter | solution.py:99
  456.0 0.7 copy-start.13
  626.6 15.7 %copy-start.1 = (bf16[1,704,2048]{2,1,0:T(8,128)(2,1)S(1)}, bf16[1,704,2048]{2,1,0:T(8,128)(2,1)}, u32[]{:S(2)}) copy-start(bf16[1,704,2048]{2,1,0:T(8,128)(2,1)} %param.35) | copy-start | bytes 8650756
  633.0 7.0 %copy-start.5 = (bf16[128,2048]{1,0:T(8,128)(2,1)S(1)}, bf16[128,2048]{1,0:T(8,128)(2,1)}, u32[]{:S(2)}) copy-start(bf16[128,2048]{1,0:T(8,128)(2,1)} %copy-done.4) | copy-start | bytes 1572868
Sparse Core Ops, SparseCore 0:
  10.9 65.0 all-gather.2
  108.2 92.0 reduce-scatter.2
  238.7 146.0 all-gather.4
  456.2 143.7 reduce-scatter.4
